TPU v7x, 128 devices: a whole 4x4x4 slice. The times are simulated.
128 devices in a mesh: dev: 128 (over x, y, z, core).
Axes of the slice: x: 4, y: 4, z: 4, core: 2. Of those that a mesh axis runs over, the one named last changes fastest.
Arguments:
- params: float32 [9, 131072], P(None, 'dev')
- moment: float32 [9, 131072], P(None, 'dev'), may hold values from -3 to 3
- second: float32 [9, 131072], P(None, 'dev'), may hold values from 0.05 to 1
- fetch_ids: int32 [128, 128, 8], P('dev'), may hold values from 0 to 1023
- seg_ids: int32 [512, 256], P('dev'), may hold values from 0 to 1023
- seg_count: int32 [512], P('dev'), may hold values from 1 to 256, 98304 in all
- seg_perm: int32 [512], replicated, may hold values from 0 to 511, as said below
- target: float32 [128, 3, 256], P('dev'), may hold values from 0 to 1
Outputs:
- image: float32 [128, 3, 256], P('dev')
- new_params: float32 [9, 131072], P(None, 'dev')
- new_moment: float32 [9, 131072], P(None, 'dev')
- new_second: float32 [9, 131072], P(None, 'dev')
Inputs may be any that keep to these rules, and one draw needn't show every extreme that they name: `seg_count`: segments that exceed their count hold unused slots; some segment is full. `seg_perm`: each number appears once.
All inputs are finite; a program needn't handle non-finite values. No bound on the sum of `seg_count` on one device may be relied on, other than what follows from the above.
Results may differ from a plain program's by a relative error of at most 0.0003.
Values sent between devices are 32-bit elements; how exact they have to be, the bound alone decides.
A program may use at most 192 MiB of HBM per device.

v0:
```python
import jax
import jax.numpy as jnp
from jax import lax
from jax.sharding import PartitionSpec as P

TILES_X = 8
KSEG = 4


def segment(par, count, tile):
    span = par.shape[1]
    pidx = jnp.arange(256, dtype=jnp.int32)
    fine_x = ((pidx % 16).astype(jnp.float32) + 0.5) / 16.0
    fine_y = ((pidx // 16).astype(jnp.float32) + 0.5) / 16.0
    pos_x = (tile % TILES_X).astype(jnp.float32) + fine_x
    pos_y = (tile // TILES_X).astype(jnp.float32) + fine_y
    steps = jnp.arange(span, dtype=jnp.int32)
    live = (steps < count).astype(jnp.float32)
    delta_x = pos_x[None, :] - par[0][:, None]
    delta_y = pos_y[None, :] - par[1][:, None]
    scale_a = jnp.exp(par[2])
    scale_c = jnp.exp(par[3])
    cross = 0.8 * jnp.tanh(par[4]) * scale_a * scale_c
    power = -0.5 * (
        (scale_a * scale_a)[:, None] * delta_x * delta_x
        + 2.0 * cross[:, None] * delta_x * delta_y
        + (scale_c * scale_c)[:, None] * delta_y * delta_y
    )
    alpha = (0.95 * jax.nn.sigmoid(par[5]) * live)[:, None] * jnp.exp(power)
    logt = jnp.log1p(-alpha)
    lower = (steps[:, None] > steps[None, :]).astype(jnp.float32)
    earlier = jnp.dot(lower, logt, precision=lax.Precision.HIGHEST)
    weight = jnp.exp(earlier) * alpha
    colour = jnp.dot(par[6:9], weight, precision=lax.Precision.HIGHEST)
    return (colour, jnp.sum(logt, axis=0))


def per_device(params, moment, second, fetch_ids, seg_ids, seg_count, seg_perm, target):
    ndev = lax.axis_size("dev")
    me = lax.axis_index("dev")
    nparam, owned = params.shape
    segs, span = seg_ids.shape
    tiles_dev = target.shape[0]
    pixels = target.shape[2]
    wanted = fetch_ids[0]
    cap = wanted.shape[1]
    received = lax.all_to_all(wanted, "dev", split_axis=0, concat_axis=0, tiled=True)
    buckets = jnp.take(params, received, axis=1)
    arrived = lax.all_to_all(buckets, "dev", split_axis=1, concat_axis=1, tiled=True)
    buffer = arrived.reshape(nparam, ndev * cap)
    first = me * segs
    own_perm = lax.dynamic_slice_in_dim(seg_perm, first, segs, 0)
    own_tile = own_perm // KSEG
    own_rank = own_perm % KSEG
    gathered_par = jnp.moveaxis(jnp.take(buffer, seg_ids, axis=1), 1, 0)

    def partials(values):
        return jax.vmap(segment)(values, seg_count, own_tile)

    (colours, logs), back = jax.vjp(partials, gathered_par)
    all_colours, all_logs, all_target = (
        lax.all_gather(colours, "dev", axis=0, tiled=True),
        lax.all_gather(logs, "dev", axis=0, tiled=True),
        lax.all_gather(target, "dev", axis=0, tiled=True),
    )
    total = all_logs.shape[0]
    ntiles = all_target.shape[0]
    tile_all = seg_perm // KSEG
    rank_all = seg_perm % KSEG
    same = tile_all[:, None] == tile_all[None, :]
    before = (same & (rank_all[None, :] < rank_all[:, None])).astype(jnp.float32)
    prefix = jnp.exp(jnp.dot(before, all_logs, precision=lax.Precision.HIGHEST))
    contrib = (prefix[:, None, :] * all_colours).reshape(total, 3 * pixels)
    onehot = (jnp.arange(ntiles, dtype=jnp.int32)[:, None] == tile_all[None, :]).astype(jnp.float32)
    image = jnp.dot(onehot, contrib, precision=lax.Precision.HIGHEST)
    misfit = image - all_target.reshape(ntiles, 3 * pixels)
    later = (
        (own_tile[:, None] == tile_all[None, :]) & (rank_all[None, :] > own_rank[:, None])
    ).astype(jnp.float32)
    behind = jnp.dot(later, contrib, precision=lax.Precision.HIGHEST).reshape(segs, 3, pixels)
    picker = (own_tile[:, None] == jnp.arange(ntiles, dtype=jnp.int32)[None, :]).astype(jnp.float32)
    error = jnp.dot(picker, misfit, precision=lax.Precision.HIGHEST).reshape(segs, 3, pixels)
    own_prefix = lax.dynamic_slice_in_dim(prefix, first, segs, 0)
    d_colour = own_prefix[:, None, :] * error
    d_log = jnp.sum(error * behind, axis=1)
    (d_par,) = back((d_colour, d_log))
    slot_grad = (
        jnp.zeros((nparam, ndev * cap), jnp.float32)
        .at[:, seg_ids.reshape(-1)]
        .add(jnp.moveaxis(d_par, 1, 0).reshape(nparam, segs * span))
    )
    owner_base = jnp.arange(ndev, dtype=jnp.int32)[:, None] * owned
    global_ids = (owner_base + wanted).reshape(-1)
    dense = jnp.zeros((nparam, ndev * owned), jnp.float32).at[:, global_ids].add(slot_grad)
    grad = lax.psum_scatter(dense, "dev", scatter_dimension=1, tiled=True)
    new_moment = 0.9 * moment + 0.1 * grad
    new_second = 0.99 * second + 0.01 * grad * grad
    new_params = params - 0.05 * new_moment / (jnp.sqrt(new_second) + 1e-08)
    my_image = lax.dynamic_slice_in_dim(image, me * tiles_dev, tiles_dev, 0).reshape(
        tiles_dev, 3, pixels
    )
    return (my_image, new_params, new_moment, new_second)


def solution(mesh):
    placed = (
        P(None, "dev"),
        P(None, "dev"),
        P(None, "dev"),
        P("dev", None, None),
        P("dev", None),
        P("dev"),
        P(),
        P("dev", None, None),
    )
    return jax.shard_map(
        per_device,
        mesh=mesh,
        in_specs=placed,
        out_specs=(P("dev", None, None), P(None, "dev"), P(None, "dev"), P(None, "dev")),
        check_vma=False,
    )
```

profile of v0, /device:TPU:1, one launch (start us, length us, event | category | flops | bytes accessed | tf_op | source)
XLA Modules:
  0.0 886.5 jit_solution(13261583860263661293)
XLA Ops:
  7.2 1.4 copy.74
  8.6 11.5 %all-to-all-start = ((s32[128,1,8]{2,1,0:T(1,128)}), s32[128,1,8]{2,1,0:T(1,128)S(1)}, u32[]{:S(2)}, u32[]{:S(2)}) async-start(s32[128,1,8]{2,1,0:T(1,128)} %bitcast), calls=%async_computation | async-start | bytes 131072 | tf_op jit(solution)/shard_map/all_to_all | solution.py:47
  20.1 0.7 compare_and_fusion.1
  20.8 0.7 fusion.95
  21.5 0.8 and_select_fusion
  22.2 0.8 fusion.105
  23.0 0.1 broadcast_add_fusion.1
  23.1 1.1 copy.75
  24.2 5.2 all-to-all-done
  29.4 0.1 reshape.393
  29.5 2.8 gather_fusion
  32.4 1.0 fusion.47
  33.4 4.8 all-to-all-start.1
  38.2 13.5 %all-to-all-done.1 = f32[9,128,8]{0,2,1:T(8,128)S(1)} async-done(((f32[9,128,8]{0,2,1:T(8,128)}), f32[9,128,8]{0,2,1:T(8,128)S(1)}, u32[]{:S(2)}, u32[]{:S(2)}) %all-to-all-start.1) | async-done | bytes 36896 | tf_op jit(solution)/shard_map/all_to_all | solution.py:49
  51.7 2.8 gather_fusion.1
  54.5 0.2 copy.77
  54.8 0.1 bitcast_select_fusion.1
  54.9 1.5 convolution_exponential_fusion
  56.4 2.1 fusion.64
  58.6 0.9 squeeze.2
  59.5 0.1 add.249
  59.6 0.1 add.250
  59.7 33.6 %all_gather.11 = f32[128,3,256]{2,1,0:T(4,128)S(1)} all-gather(f32[1,3,256]{2,1,0:T(4,128)S(1)} %copy.82), channel_id=1, replica_groups=mesh['dev'=128] {'dev'}, dimensions={0}, use_global_device_ids=true | all-gather | bytes 396288 | tf_op jit(solution)/shard_map/all_gather | solution.py:64
  93.4 0.2 copy.83
  93.6 0.2 copy.84
  93.8 3.8 sort
  97.6 1.0 log-plus-one_reduce_fusion
  98.6 35.8 %all-gather = f32[128,4,256]{2,1,0:T(4,128)S(1)} all-gather(f32[1,4,256]{2,1,0:T(4,128)S(1)} %bitcast.124), channel_id=1, replica_groups=mesh['dev'=128] {'dev'}, dimensions={0}, use_global_device_ids=true | all-gather | bytes 528384 | tf_op jit(solution)/shard_map/all_gather | solution.py:63
  134.4 0.2 reshape.427
  134.6 0.7 convolution_exponential_fusion.1
  135.3 0.2 copy.78
  135.6 1.8 copy.80
  137.4 0.2 broadcast_multiply_fusion
  137.7 1.0 fusion.69
  138.7 0.3 fusion.65
  139.0 1.2 fusion.63
  140.2 1.0 fusion.75
  141.2 0.8 fusion.15
  142.0 3.0 fusion.36
  145.1 0.1 fusion.84
  145.2 0.1 add_bitcast_fusion
  145.3 0.2 copy.89
  145.6 6.4 scatter_custom_fusion
  151.9 42.3 %scatter_custom_fusion.1 = f32[9,131072]{0,1:T(8,128)} fusion(s32[1024]{0:T(1024)S(1)} %get-tuple-element.16, f32[]{:T(128)} %constant.152.clone.1, f32[1024,9]{1,0:T(8,128)S(1)} %bitcast.115, s32[1024]{0:T(1024)S(1)} %broadcast_clamp_fusion), kind=kCustom, calls=%fused_computation.5 | custom fusion | flops 9216 | bytes 4718596 | tf_op jit(solution)/shard_map/scatter-add | solution.py:94
  194.3 36.9 %copy.90 = f32[9,131072]{1,0:T(8,128)} copy(f32[9,131072]{0,1:T(8,128)} %scatter_custom_fusion.1) | data formatting | bytes 9437184 | tf_op jit(solution)/shard_map/scatter-add | solution.py:94
  231.2 0.6 constant_dynamic-slice_fusion.1
  231.8 646.4 %reduce-scatter.2.cloned.1.call-done = f32[9,1024]{1,0:T(8,128)} async-done(((f32[9,131072]{1,0:T(8,128)}), f32[9,1024]{1,0:T(8,128)}) %reduce-scatter.2.cloned.1.call-update) | async-done | bytes 36880 | tf_op jit(solution)/shard_map/reduce_scatter | solution.py:95
  878.2 1.5 divide_subtract_fusion
  (55 shorter events, 0.5 us)
Async XLA Ops:
  8.6 20.8 %all-to-all-start = ((s32[128,1,8]{2,1,0:T(1,128)}), s32[128,1,8]{2,1,0:T(1,128)S(1)}, u32[]{:S(2)}, u32[]{:S(2)}) async-start(s32[128,1,8]{2,1,0:T(1,128)} %bitcast), calls=%async_computation | async-start | bytes 131072 | tf_op jit(solution)/shard_map/all_to_all | solution.py:47
  32.4 22.4 %copy-start.6 = (s32[4]{0:T(128)S(1)}, s32[4]{0:T(128)}, u32[]{:S(2)}) copy-start(s32[4]{0:T(128)} %param.13) | copy-start | bytes 52
  33.4 18.3 %all-to-all-start.1 = ((f32[9,128,8]{0,2,1:T(8,128)}), f32[9,128,8]{0,2,1:T(8,128)S(1)}, u32[]{:S(2)}, u32[]{:S(2)}) async-start(f32[9,128,8]{0,2,1:T(8,128)} %fusion.47), calls=%async_computation.1 | async-start | bytes 1048576 | tf_op jit(solution)/shard_map/all_to_all | solution.py:49
  38.1 97.5 %all-gather.3.cloned.1.call-start = ((), (), s32[]{:S(2)}) async-start(), calls=%async_computation.3 | async-start | bytes 2113536 | tf_op jit(solution)/shard_map/all_gather | solution.py:62
  56.3 2.1 copy-start.7
  56.4 3.1 copy-start.5
  56.4 3.2 copy-start.3
  58.5 39.1 %copy-start.4 = (s32[512]{0:T(512)S(1)}, s32[512]{0:T(512)}, u32[]{:S(2)}) copy-start(s32[512]{0:T(512)} %param.14) | copy-start | bytes 6148
  58.5 819.7 %reduce-scatter.2.cloned.1.call-start = ((), (), s32[]{:S(2)}) async-start(), calls=%async_computation.4 | async-start | bytes 8454144 | tf_op jit(solution)/shard_map/reduce_scatter | solution.py:95
  137.7 1.3 copy-start.8
  231.2 647.0 %copy-start = (f32[9,1024]{1,0:T(8,128)S(1)}, f32[9,1024]{1,0:T(8,128)}, u32[]{:S(2)}) copy-start(f32[9,1024]{1,0:T(8,128)} %param.8) | copy-start | bytes 110596
  231.2 647.0 %copy-start.1 = (f32[9,1024]{1,0:T(8,128)S(1)}, f32[9,1024]{1,0:T(8,128)}, u32[]{:S(2)}) copy-start(f32[9,1024]{1,0:T(8,128)} %param.9) | copy-start | bytes 110596
  231.2 647.0 %copy-start.2 = (f32[9,1024]{1,0:T(8,128)S(1)}, f32[9,1024]{1,0:T(8,128)}, u32[]{:S(2)}) copy-start(f32[9,1024]{1,0:T(8,128)} %param.10) | copy-start | bytes 110596
Sparse Core Ops, SparseCore 0:
  58.6 63.3 all-gather.2
  231.3 646.7 reduce-scatter.1
where the time goes:
time: 894 us; the launch traced here: 887 us
  waiting for transfers between devices  665 us (74%)
  blocking collectives  69.4 us (8%)
  other arithmetic  59.6 us (7%)
  local copies, waits for them, and re-layouts  49.9 us (6%)
  starting transfers between devices  16.3 us (2%)
  between operations  14.5 us (2%)
  matrix products  11.6 us (1%)
    reduce_scatter x1, waiting for transfers between devices, per_device(): grad = lax.psum_scatter(dense, 'dev', scatter_dimension=1, tiled=True)  646 us
    scatter-add x3, other arithmetic, per_device(): jnp.zeros((nparam, ndev * owned), jnp.float32).at[:, global_ids]  46.1 us
    scatter-add x2, local copies, waits for them, and re-layouts, per_device(): jnp.zeros((nparam, ndev * owned), jnp.float32).at[:, global_ids]  36.9 us
    all_gather x1, blocking collectives, per_device(): lax.all_gather(logs, 'dev', axis=0, tiled=True)  35.8 us
    all_gather x1, blocking collectives, per_device(): lax.all_gather(target, 'dev', axis=0, tiled=True)  33.6 us
  transfers between devices with their start and end apart: 4, of which 3 were waited for; matrix products, arithmetic and copies ran while one was open for 1% of the time, Pallas kernels for 0%

commit v1 on v0

--- a/solution.py
+++ b/solution.py
@@ -89,10 +89,14 @@
         .at[:, seg_ids.reshape(-1)]
         .add(jnp.moveaxis(d_par, 1, 0).reshape(nparam, segs * span))
     )
-    owner_base = jnp.arange(ndev, dtype=jnp.int32)[:, None] * owned
-    global_ids = (owner_base + wanted).reshape(-1)
-    dense = jnp.zeros((nparam, ndev * owned), jnp.float32).at[:, global_ids].add(slot_grad)
-    grad = lax.psum_scatter(dense, "dev", scatter_dimension=1, tiled=True)
+    returned = lax.all_to_all(
+        slot_grad.reshape(nparam, ndev, cap), "dev", split_axis=1, concat_axis=1, tiled=True
+    )
+    grad = (
+        jnp.zeros((nparam, owned), jnp.float32)
+        .at[:, received.reshape(-1)]
+        .add(returned.reshape(nparam, ndev * cap))
+    )
     new_moment = 0.9 * moment + 0.1 * grad
     new_second = 0.99 * second + 0.01 * grad * grad
     new_params = params - 0.05 * new_moment / (jnp.sqrt(new_second) + 1e-08)

time: 894 us -> 181 us (0.20)
  waiting for transfers between devices: 665 us -> 31.7 us
  other arithmetic: 59.6 us -> 20.1 us
  local copies, waits for them, and re-layouts: 49.9 us -> 12.7 us
    reduce_scatter x1 -> x0, waiting for transfers between devices: 646 us -> none  [per_device(): grad = lax.psum_scatter(dense, 'dev', scatter_dimension=1, tiled=True)]
    scatter-add x3 -> x1, other arithmetic: 46.1 us -> 6.18 us  [per_device(): grad = jnp.zeros((nparam, owned), jnp.float32).at[:, received.reshape(-1)...]
    scatter-add x2 -> x1, local copies, waits for them, and re-layouts: 36.9 us -> 0.19 us  [per_device(): grad = jnp.zeros((nparam, owned), jnp.float32).at[:, received.reshape(-1)...]
    all_to_all x0 -> x1, waiting for transfers between devices: none -> 13 us  [per_device(): lax.all_to_all(slot_grad.reshape(nparam, ndev, cap), 'dev', split_axis=1,...]
  transfers between devices with their start and end apart: 4 -> 4, of which waited for: 3 -> 3; matrix products, arithmetic and copies ran while one was open for 1% -> 5% of each run, Pallas kernels for 0% -> 0%
where the time goes in v1:
time: 181 us
  blocking collectives  69.2 us (38%)
  waiting for transfers between devices  31.7 us (18%)
  starting transfers between devices  20.9 us (12%)
  other arithmetic  20.1 us (11%)
  between operations  14.5 us (8%)
  local copies, waits for them, and re-layouts  12.7 us (7%)
  matrix products  11.7 us (6%)
    all_gather x1, blocking collectives, per_device(): lax.all_gather(logs, 'dev', axis=0, tiled=True)  35.5 us
    all_gather x1, blocking collectives, per_device(): lax.all_gather(target, 'dev', axis=0, tiled=True)  33.7 us
    all_to_all x1, waiting for transfers between devices, per_device(): lax.all_to_all(buckets, 'dev', split_axis=1, concat_axis=1, tiled=True)  13.5 us
    all_to_all x1, waiting for transfers between devices, per_device(): lax.all_to_all(slot_grad.reshape(nparam, ndev, cap), 'dev', split_axis=1,...  13 us
    all_to_all x1, starting transfers between devices, per_device(): lax.all_to_all(wanted, 'dev', split_axis=0, concat_axis=0, tiled=True)  11.5 us
    scatter-add x1, other arithmetic, per_device(): slot_grad = jnp.zeros((nparam, ndev * cap), jnp.float32).at[:, seg_ids.re...  6.79 us
    scatter-add x1, other arithmetic, per_device(): grad = jnp.zeros((nparam, owned), jnp.float32).at[:, received.reshape(-1)...  6.18 us
    all_to_all x1, waiting for transfers between devices, per_device(): lax.all_to_all(wanted, 'dev', split_axis=0, concat_axis=0, tiled=True)  5.21 us
  transfers between devices with their start and end apart: 4, of which 3 were waited for; matrix products, arithmetic and copies ran while one was open for 5% of the time, Pallas kernels for 0%

profile of v1, /device:TPU:1, one launch (start us, length us, event | category | flops | bytes accessed | tf_op | source)
XLA Modules:
  0.0 180.8 jit_solution(5734400977405865448)
XLA Ops:
  7.2 1.4 copy.73
  8.6 11.5 %all-to-all-start = ((s32[128,1,8]{2,1,0:T(1,128)}), s32[128,1,8]{2,1,0:T(1,128)S(1)}, u32[]{:S(2)}, u32[]{:S(2)}) async-start(s32[128,1,8]{2,1,0:T(1,128)} %bitcast), calls=%async_computation | async-start | bytes 131072 | tf_op jit(solution)/shard_map/all_to_all | solution.py:47
  20.1 0.7 fusion.92
  20.8 0.7 compare_and_fusion.1
  21.5 0.8 and_select_fusion
  22.3 0.8 fusion.102
  23.0 0.1 broadcast_add_fusion.1
  23.1 1.1 copy.74
  24.2 5.2 %all-to-all-done = s32[128,1,8]{2,1,0:T(1,128)S(1)} async-done(((s32[128,1,8]{2,1,0:T(1,128)}), s32[128,1,8]{2,1,0:T(1,128)S(1)}, u32[]{:S(2)}, u32[]{:S(2)}) %all-to-all-start) | async-done | bytes 4128 | tf_op jit(solution)/shard_map/all_to_all | solution.py:47
  29.4 0.1 reshape.400
  29.5 2.8 %gather_fusion = f32[1024,9]{1,0:T(8,128)S(1)} fusion(f32[9,1024]{0,1:T(8,128)S(1)} %copy.74, s32[1024]{0:T(1024)S(1)} %broadcast_clamp_fusion.1), kind=kCustom, calls=%fused_computation | custom fusion | bytes 77824 | tf_op jit(solution)/shard_map/jit(_take)/gather | solution.py:48
  32.4 1.0 fusion.43
  33.4 4.8 %all-to-all-start.1 = ((f32[9,128,8]{0,2,1:T(8,128)}), f32[9,128,8]{0,2,1:T(8,128)S(1)}, u32[]{:S(2)}, u32[]{:S(2)}) async-start(f32[9,128,8]{0,2,1:T(8,128)} %fusion.43), calls=%async_computation.1 | async-start | bytes 1048576 | tf_op jit(solution)/shard_map/all_to_all | solution.py:49
  38.2 13.5 %all-to-all-done.1 = f32[9,128,8]{0,2,1:T(8,128)S(1)} async-done(((f32[9,128,8]{0,2,1:T(8,128)}), f32[9,128,8]{0,2,1:T(8,128)S(1)}, u32[]{:S(2)}, u32[]{:S(2)}) %all-to-all-start.1) | async-done | bytes 36896 | tf_op jit(solution)/shard_map/all_to_all | solution.py:49
  51.7 2.8 %gather_fusion.1 = f32[1024,9]{1,0:T(8,128)S(1)} fusion(f32[9,1024]{0,1:T(8,128)S(1)} %bitcast.116, s32[1024]{0:T(1024)S(1)} %broadcast_clamp_fusion), kind=kCustom, calls=%fused_computation.1 | custom fusion | bytes 77824 | tf_op jit(solution)/shard_map/jit(_take)/gather | solution.py:55
  54.5 0.2 copy.76
  54.8 0.1 bitcast_select_fusion.1
  54.9 1.5 convolution_exponential_fusion
  56.4 2.1 %fusion.60 = f32[4,3,256]{2,1,0:T(4,128)} fusion(f32[256,4,256]{0,2,1:T(8,128)S(1)} %convolution_exponential_fusion, f32[4,256]{1,0:T(4,128)S(1)} %get-tuple-element.48, f32[4,256]{1,0:T(4,128)S(1)} %get-tuple-element.51, f32[4,256]{1,0:T(4,128)S(1)} %get-tuple-element.56, f32[4,256]{1,0:T(4,128)S(1)} %get-tuple-element.44, ...), kind=kOutput, calls=%fused_computation.86 | convolution fusion | flops 12845056 | bytes 1110016 | tf_op jit(solution)/shard_map/jvp(vmap())/dot_general | solution.py:34
  58.5 33.7 %all_gather.11 = f32[128,3,256]{2,1,0:T(4,128)S(1)} all-gather(f32[1,3,256]{2,1,0:T(4,128)S(1)} %copy.80), channel_id=1, replica_groups=mesh['dev'=128] {'dev'}, dimensions={0}, use_global_device_ids=true | all-gather | bytes 396288 | tf_op jit(solution)/shard_map/all_gather | solution.py:64
  92.3 0.2 copy.81
  92.5 0.2 copy.82
  92.7 0.5 broadcast.499
  93.2 0.8 reduce.3
  94.0 0.1 reshape.387
  94.1 1.0 log-plus-one_reduce_fusion
  95.2 35.5 %all-gather = f32[128,4,256]{2,1,0:T(4,128)S(1)} all-gather(f32[1,4,256]{2,1,0:T(4,128)S(1)} %bitcast.127), channel_id=1, replica_groups=mesh['dev'=128] {'dev'}, dimensions={0}, use_global_device_ids=true | all-gather | bytes 528384 | tf_op jit(solution)/shard_map/all_gather | solution.py:63
  130.7 0.2 reshape.434
  130.9 0.7 convolution_exponential_fusion.1
  131.6 0.2 copy.77
  131.9 1.8 %copy.79 = f32[512,3,256]{0,2,1:T(8,128)S(1)} copy(f32[512,3,256]{2,1,0:T(4,128)} %all-gather.3.cloned.1.call-done) | data formatting | bytes 3145728 | tf_op jit(solution)/shard_map/all_gather | solution.py:62
  133.7 0.2 broadcast_multiply_fusion
  133.9 1.0 fusion.66
  135.0 0.3 fusion.61
  135.2 1.1 fusion.72
  136.3 1.2 fusion.59
  137.5 0.8 fusion.12
  138.3 3.0 %fusion.33 = (f32[4,256]{1,0:T(4,128)S(1)}, f32[4,256]{1,0:T(4,128)S(1)}, f32[4,256]{1,0:T(4,128)S(1)}, f32[4,256]{1,0:T(4,128)S(1)}, f32[4,256]{1,0:T(4,128)S(1)}, /*index=5*/f32[4,256]{1,0:T(4,128)S(1)}) fusion(f32[4,256]{1,0:T(4,128)S(1)} %get-tuple-element.51, f32[4,256]{1,0:T(4,128)S(1)} %get-tuple-element.56, f32[4,256]{1,0:T(4,128)S(1)} %get-tuple-element.48, ...), kind=kOutput, calls=%fused_computation.52 | convolution fusion | flops 820570112 | bytes 2183168 | tf_op jit(solution)/shard_map/transpose(jvp(vmap()))/dot_general | solution.py:32
  141.4 0.1 fusion.81
  141.5 0.1 add_bitcast_fusion
  141.7 0.2 copy.87
  141.9 6.8 %scatter_custom_fusion = f32[9,1024]{0,1:T(8,128)} fusion(s32[1024]{0:T(1024)S(1)} %bitcast.130, f32[1024,9]{1,0:T(8,128)S(1)} %copy.87, f32[]{:T(128)} %constant.149.clone.1), kind=kCustom, calls=%fused_computation.90 | custom fusion | flops 9216 | bytes 36868 | tf_op jit(solution)/shard_map/scatter-add | solution.py:90
  148.7 4.6 %all-to-all-start.2 = ((f32[9,128,8]{0,2,1:T(8,128)}), f32[9,128,8]{0,2,1:T(8,128)S(1)}, u32[]{:S(2)}, u32[]{:S(2)}) async-start(f32[9,128,8]{0,2,1:T(8,128)} %bitcast.30), calls=%async_computation.2 | async-start | bytes 1048576 | tf_op jit(solution)/shard_map/all_to_all | solution.py:92
  153.4 0.6 constant_dynamic-slice_fusion.1
  154.0 13.0 %all-to-all-done.2 = f32[9,128,8]{0,2,1:T(8,128)S(1)} async-done(((f32[9,128,8]{0,2,1:T(8,128)}), f32[9,128,8]{0,2,1:T(8,128)S(1)}, u32[]{:S(2)}, u32[]{:S(2)}) %all-to-all-start.2) | async-done | bytes 36896 | tf_op jit(solution)/shard_map/all_to_all | solution.py:92
  166.9 6.2 %scatter_custom_fusion.1 = f32[9,1024]{0,1:T(8,128)S(1)} fusion(s32[1024]{0:T(1024)S(1)} %bitcast.129, f32[9,128,8]{0,2,1:T(8,128)S(1)} %all-to-all-done.2, f32[]{:T(128)} %constant.149.clone.1), kind=kCustom, calls=%fused_computation.67 | custom fusion | flops 9216 | bytes 561156 | tf_op jit(solution)/shard_map/scatter-add | solution.py:98
  173.1 0.2 copy.88
  173.3 0.7 divide_subtract_fusion
  (50 shorter events, 0.4 us)
Async XLA Ops:
  8.6 20.8 %all-to-all-start = ((s32[128,1,8]{2,1,0:T(1,128)}), s32[128,1,8]{2,1,0:T(1,128)S(1)}, u32[]{:S(2)}, u32[]{:S(2)}) async-start(s32[128,1,8]{2,1,0:T(1,128)} %bitcast), calls=%async_computation | async-start | bytes 131072 | tf_op jit(solution)/shard_map/all_to_all | solution.py:47
  32.3 22.4 %copy-start.6 = (s32[4]{0:T(128)S(1)}, s32[4]{0:T(128)}, u32[]{:S(2)}) copy-start(s32[4]{0:T(128)} %param.13) | copy-start | bytes 52
  33.4 18.3 %all-to-all-start.1 = ((f32[9,128,8]{0,2,1:T(8,128)}), f32[9,128,8]{0,2,1:T(8,128)S(1)}, u32[]{:S(2)}, u32[]{:S(2)}) async-start(f32[9,128,8]{0,2,1:T(8,128)} %fusion.43), calls=%async_computation.1 | async-start | bytes 1048576 | tf_op jit(solution)/shard_map/all_to_all | solution.py:49
  38.1 93.7 %all-gather.3.cloned.1.call-start = ((), (), s32[]{:S(2)}) async-start(), calls=%async_computation.3 | async-start | bytes 2113536 | tf_op jit(solution)/shard_map/all_gather | solution.py:62
  56.3 2.1 %copy-start.7 = (f32[256,4,256]{0,2,1:T(8,128)}, f32[256,4,256]{0,2,1:T(8,128)S(1)}, u32[]{:S(2)}) copy-start(f32[256,4,256]{0,2,1:T(8,128)S(1)} %convolution_exponential_fusion) | copy-start | bytes 3145732
  56.4 2.2 %copy-start.3 = (s32[4,256]{1,0:T(4,128)S(1)}, s32[4,256]{1,0:T(4,128)}, u32[]{:S(2)}) copy-start(s32[4,256]{1,0:T(4,128)} %param.12) | copy-start | bytes 12292
  56.4 2.2 %copy-start.5 = (f32[1,3,256]{2,0,1:T(1,128)S(1)}, f32[1,3,256]{2,0,1:T(1,128)}, u32[]{:S(2)}) copy-start(f32[1,3,256]{2,0,1:T(1,128)} %param.15) | copy-start | bytes 9220
  58.5 34.2 %copy-start.4 = (s32[512]{0:T(512)S(1)}, s32[512]{0:T(512)}, u32[]{:S(2)}) copy-start(s32[512]{0:T(512)} %param.14) | copy-start | bytes 6148
  133.9 2.4 %copy-start.8 = (f32[256,4,256]{0,2,1:T(8,128)S(1)}, f32[256,4,256]{0,2,1:T(8,128)}, u32[]{:S(2)}) copy-start(f32[256,4,256]{0,2,1:T(8,128)} %copy-done.7) | copy-start | bytes 3145732
  141.9 31.4 %copy-start = (f32[9,1024]{1,0:T(8,128)S(1)}, f32[9,1024]{1,0:T(8,128)}, u32[]{:S(2)}) copy-start(f32[9,1024]{1,0:T(8,128)} %param.8) | copy-start | bytes 110596
  141.9 31.4 %copy-start.1 = (f32[9,1024]{1,0:T(8,128)S(1)}, f32[9,1024]{1,0:T(8,128)}, u32[]{:S(2)}) copy-start(f32[9,1024]{1,0:T(8,128)} %param.9) | copy-start | bytes 110596
  141.9 31.4 %copy-start.2 = (f32[9,1024]{1,0:T(8,128)S(1)}, f32[9,1024]{1,0:T(8,128)}, u32[]{:S(2)}) copy-start(f32[9,1024]{1,0:T(8,128)} %param.10) | copy-start | bytes 110596
  148.7 18.2 %all-to-all-start.2 = ((f32[9,128,8]{0,2,1:T(8,128)}), f32[9,128,8]{0,2,1:T(8,128)S(1)}, u32[]{:S(2)}, u32[]{:S(2)}) async-start(f32[9,128,8]{0,2,1:T(8,128)} %bitcast.30), calls=%async_computation.2 | async-start | bytes 1048576 | tf_op jit(solution)/shard_map/all_to_all | solution.py:92
Sparse Core Ops, SparseCore 0:
  58.6 62.3 all-gather.2

commit v2 on v0

v2 whole, which is shorter than its diff:
```python
import jax
import jax.numpy as jnp
from jax import lax
from jax.experimental import pallas as pl
from jax.experimental.pallas import tpu as pltpu
from jax.sharding import PartitionSpec as P

F32, BF16, I32 = jnp.float32, jnp.bfloat16, jnp.int32
MESH = pl.DeviceIdType.MESH
N = 128
SEGS = 4
SPAN = 256
PIX = 256
CHUNK = 32
CHUNKS = PIX // CHUNK
CAP = 8


def iota(shape, axis):
    return lax.broadcasted_iota(I32, shape, axis)


def onehot(cond):
    return jnp.where(cond, 1.0, 0.0).astype(BF16)


def mm(a, b):
    return jnp.dot(a, b, preferred_element_type=F32)


def split2(x):
    hi = x.astype(BF16)
    lo = (x - hi.astype(F32)).astype(BF16)
    return hi, lo


def split3(x):
    hi = x.astype(BF16)
    rest = x - hi.astype(F32)
    mid = rest.astype(BF16)
    lo = (rest - mid.astype(F32)).astype(BF16)
    return hi, mid, lo


def exact_rows(x, sel):
    n = x.shape[0]
    pad = -n % 16
    if pad:
        x = jnp.concatenate([x, jnp.zeros((pad, x.shape[1]), F32)], axis=0)
    out = mm(jnp.concatenate(split3(x), axis=0), sel)
    m = n + pad
    return (out[:n] + out[m : m + n]) + out[2 * m : 2 * m + n]


def pick(table, sel, high):
    got = exact_rows(table, sel)
    main = jnp.zeros((8, got.shape[1]), F32)
    for h in range(8):
        main = main + jnp.where(high == h, got[8 * h : 8 * h + 8], 0.0)
    last = jnp.where(iota((8, got.shape[1]), 0) == high, got[64:72], 0.0)
    return main, jnp.sum(last, axis=0, keepdims=True)


def spread(main, last, high, sel):
    rows = [jnp.where(high == h, main, 0.0) for h in range(8)]
    rows.append(jnp.where(iota(main.shape, 0) == high, last, 0.0))
    rows.append(jnp.zeros_like(main))
    x = jnp.concatenate(rows, axis=0)
    out = mm(jnp.concatenate(split2(x), axis=0), sel)
    return out[:72] + out[80:152]


def pad_rows(x):
    return jnp.concatenate([x, jnp.zeros((N - x.shape[0], x.shape[1]), F32)], axis=0)


def kernel(
    count_ref, perm_ref, par_ref, mom_ref, sec_ref, fetch_ref, ids_ref, permv_ref, tgt_ref,
    img_ref, npar_ref, nmom_ref, nsec_ref,
    send_buf, recv_buf, e_ref, et_ref, o_ref, ot_ref, ohj_ref, rows_ref, f_ref, q_ref,
    a_ref, w_ref, hi_ref, lo_ref, x_ref, dp_ref, dpl_ref,
    send_sem, recv_sem,
):
    me = lax.axis_index("dev")
    barrier = pltpu.get_barrier_semaphore()

    def greet(i, _):
        pl.semaphore_signal(
            barrier, inc=1, device_id=(lax.rem(me + i, N),), device_id_type=MESH
        )
        return 0

    lax.fori_loop(1, N, greet, 0)

    def send(r):
        def one(i, _):
            to = lax.rem(me + i, N)
            pltpu.make_async_remote_copy(
                src_ref=send_buf.at[r, pl.ds(to, 1)],
                dst_ref=recv_buf.at[r, pl.ds(me, 1)],
                send_sem=send_sem.at[r],
                recv_sem=recv_sem.at[r],
                device_id=(to,),
                device_id_type=MESH,
            ).start()
            return 0

        lax.fori_loop(1, N, one, 0)
        pltpu.make_async_copy(
            send_buf.at[r, pl.ds(me, 1)], recv_buf.at[r, pl.ds(me, 1)], recv_sem.at[r]
        ).start()

    def receive(r):
        pltpu.make_async_copy(send_buf.at[r], recv_buf.at[r], recv_sem.at[r]).wait()
        return recv_buf[r]

    send_buf[0] = pad_rows(fetch_ref[...].astype(F32)).T
    pl.semaphore_wait(barrier, N - 1)
    send(0)

    ids = [ids_ref[s : s + 1, :] for s in range(SEGS)]
    for s in range(SEGS):
        for h in range(2):
            row = jnp.broadcast_to(ids[s][:, h * N : (h + 1) * N] // CAP, (N, N))
            at = (2 * s + h) * N
            sel = jnp.where(iota((N, N), 0) == row, 1.0, 0.0)
            et_ref[:, at : at + N] = sel.astype(BF16)
            e_ref[at : at + N, :] = sel.T.astype(BF16)
    slot = jnp.concatenate(ids, axis=1) % CAP
    table = [par_ref[0:8, c * N : (c + 1) * N] for c in range(8)]
    table += [par_ref[8:9, c * N : (c + 1) * N] for c in range(8)]
    table = jnp.concatenate(table, axis=0)

    got = receive(0).astype(I32)
    wanted = got.astype(F32).T[0:8].astype(I32)
    wanted = jnp.concatenate([wanted[k : k + 1] for k in range(CAP)], axis=1)
    high = wanted // N
    low = wanted % N
    oht = onehot(iota((N, CAP * N), 0) == low)
    main, last = pick(table, oht, high)
    out = [main[:, k * N : (k + 1) * N] for k in range(CAP)]
    out += [last[:, k * N : (k + 1) * N] for k in range(CAP)]
    send_buf[1] = pad_rows(jnp.concatenate(out, axis=0)).T
    send(1)

    lane = iota((N, N), 1)
    for k in range(CAP):
        ohj_ref[k * N : (k + 1) * N, :] = onehot(got[:, k : k + 1] % N == lane)
    nat = permv_ref[...]
    nat = jnp.concatenate([nat // SEGS, nat % SEGS], axis=0).astype(F32).astype(BF16)
    col = iota((N, SEGS * N), 1)
    deal = mm(nat_pad(nat), onehot(iota((N, SEGS * N), 0) == 4 * (col % 32) + col // N))
    quarter = (iota((1, SEGS * N), 1) % N) // 32
    code = jnp.zeros((1, SEGS * N), F32)
    for a in range(4):
        code = code + jnp.where(
            quarter == a, deal[a : a + 1] + N * deal[4 + a : 5 + a], 0.0
        )
    for b in range(4):
        piece = jnp.broadcast_to(code[:, b * N : (b + 1) * N].astype(I32), (N, N))
        for k in range(4):
            sel = jnp.where(iota((N, N), 0) + k * N == piece, 1.0, 0.0)
            o_ref[k * N : (k + 1) * N, b * N : (b + 1) * N] = sel.astype(BF16)
            ot_ref[b * N : (b + 1) * N, k * N : (k + 1) * N] = sel.T.astype(BF16)
    tgt = []
    for h in range(2):
        tgt += [tgt_ref[ch, :, h * N : (h + 1) * N] for ch in range(3)]
        tgt.append(jnp.zeros((1, N), F32))
    tgt = jnp.concatenate([jnp.zeros((32, N), F32)] + tgt, axis=0)
    f_ref[...] = pad_rows(tgt).T

    arrived = receive(1).T
    main, last = pick(arrived[0:72], et_ref[...], slot)
    scale = jnp.exp(main)
    bend = jnp.tanh(main)
    gate = jax.nn.sigmoid(main)
    sa, sc = scale[2:3], scale[3:4]
    th, sg = bend[4:5], gate[5:6]
    cross = 0.8 * th * sa * sc
    step = iota((1, SPAN), 1)
    live = jnp.concatenate(
        [jnp.where(step < count_ref[s], 1.0, 0.0) for s in range(SEGS)], axis=1
    )
    rows = [
        main[0:1], main[1:2], -0.5 * (sa * sa), -cross, -0.5 * (sc * sc), 0.95 * sg * live,
        main[6:7], main[7:8], last, 0.8 * (1.0 - th * th) * sa * sc, 1.0 - sg,
    ]
    for s in range(SEGS):
        for i, row in enumerate(rows):
            rows_ref[s, i : i + 1, :] = row[:, s * SPAN : (s + 1) * SPAN]

    def tile_of(s):
        tile = perm_ref[me * SEGS + s] // SEGS
        return (tile % 8).astype(F32), (tile // 8).astype(F32)

    def row(s, i):
        return rows_ref[s, i : i + 1, :]

    fine_x = (iota((16, SPAN), 0).astype(F32) + 0.5) / 16.0

    def delta_x(s):
        return (tile_of(s)[0] + fine_x) - row(s, 0)

    def delta_y(s, line):
        at = tile_of(s)[1] + (line.astype(F32) + 0.5) / 16.0
        return at - row(s, 1)

    def twice(x):
        return jnp.concatenate([x, x], axis=0)

    def lines(s, c):
        return jnp.concatenate(
            [jnp.broadcast_to(delta_y(s, 2 * c + i), (16, SPAN)) for i in range(2)], axis=0
        )

    def place(s, c):
        return pl.ds(pl.multiple_of(s * PIX + c * CHUNK, CHUNK), CHUNK)

    lane32 = iota((CHUNK, N), 1)

    def forward_a(s, _):
        dx = delta_x(s)
        t1 = twice(row(s, 2) * dx * dx)
        t2 = twice(row(s, 3) * dx)

        def one(c, _):
            dy = lines(s, c)
            alpha = row(s, 5) * jnp.exp(t1 + dy * (t2 + row(s, 4) * dy))
            logt = jnp.log(1.0 - alpha)
            at = place(s, c)
            a_ref[at, :] = alpha
            hi, lo = split2(logt)
            hi_ref[at, :] = hi
            lo_ref[at, :] = lo
            total = jnp.sum(logt, axis=1, keepdims=True)
            q = pl.ds(pl.multiple_of(lax.rem(c, 4) * CHUNK, CHUNK), CHUNK)
            f_ref[q, :] = jnp.where(
                lane32 == 8 * s + 4 * (c // 4) + 3, total, f_ref[q, :]
            )
            return 0

        return lax.fori_loop(0, CHUNKS, one, 0)

    lax.fori_loop(0, SEGS, forward_a, 0)

    tri = iota((SPAN, SPAN), 0) < iota((SPAN, SPAN), 1)
    earlier = onehot(tri)

    def sums(s, _):
        at = pl.ds(pl.multiple_of(s * PIX, PIX), PIX)
        x_ref[at, :] = mm(hi_ref[at, :], earlier) + mm(lo_ref[at, :], earlier)
        return 0

    lax.fori_loop(0, SEGS, sums, 0)

    def forward_b(s, _):
        def one(c, _):
            at = place(s, c)
            alpha = a_ref[at, :]
            weight = jnp.exp(x_ref[at, :]) * alpha
            w_ref[at, :] = weight
            a_ref[at, :] = alpha / (1.0 - alpha)
            q = pl.ds(pl.multiple_of(lax.rem(c, 4) * CHUNK, CHUNK), CHUNK)
            kept = f_ref[q, :]
            for ch in range(3):
                total = jnp.sum(weight * row(s, 6 + ch), axis=1, keepdims=True)
                kept = jnp.where(lane32 == 8 * s + 4 * (c // 4) + ch, total, kept)
            f_ref[q, :] = kept
            return 0

        return lax.fori_loop(0, CHUNKS, one, 0)

    lax.fori_loop(0, SEGS, forward_b, 0)

    send_buf[2] = f_ref[...]
    send(2)
    seen = receive(2).T
    by_seg = jnp.concatenate([seen[8 * s : 8 * s + 8] for s in range(SEGS)], axis=1)
    target = seen[32:40]
    by_tile = exact_rows(by_seg, ot_ref[...])
    sub = iota((8, N), 0) % 4
    colour = sub < 3
    before = jnp.zeros((8, N), F32)
    image = jnp.zeros((8, N), F32)
    terms = []
    for k in range(4):
        part = by_tile[:, k * N : (k + 1) * N]
        through = jnp.exp(before)
        contrib = jnp.where(colour, through * part, 0.0)
        terms.append((through, contrib))
        image = image + contrib
        log = jnp.where(colour, 0.0, part)
        log = log + pltpu.roll(log, 7, 0)
        before = before + (log + pltpu.roll(log, 6, 0))
    error = jnp.where(colour, image - target, 0.0)
    behind = jnp.zeros((8, N), F32)
    back = [None] * 4
    for k in (3, 2, 1, 0):
        through, contrib = terms[k]
        z = error * behind
        z = pltpu.roll(z, 1, 0) + (pltpu.roll(z, 2, 0) + pltpu.roll(z, 3, 0))
        back[k] = jnp.where(colour, through * error, z)
        behind = behind + contrib
    by_seg = exact_rows(jnp.concatenate(back, axis=1), o_ref[...])
    out = [by_seg[:, s * N : (s + 1) * N] for s in range(SEGS)] + [image]
    send_buf[3] = pad_rows(jnp.concatenate(out, axis=0)).T
    send(3)
    q_ref[...] = receive(3)

    def backward_a(s, _):
        def one(c, acc):
            at = place(s, c)
            q = pl.ds(pl.multiple_of(lax.rem(c, 4) * CHUNK, CHUNK), CHUNK)
            mine = q_ref[q, :]
            weight = w_ref[at, :]
            d_weight = jnp.zeros((CHUNK, SPAN), F32)
            new = []
            for ch in range(3):
                d = jnp.where(lane32 == 8 * s + 4 * (c // 4) + ch, mine, 0.0)
                d = jnp.sum(d, axis=1, keepdims=True)
                d_weight = d_weight + d * row(s, 6 + ch)
                g = weight * d
                g = (g[0:8] + g[8:16]) + (g[16:24] + g[24:32])
                new.append(acc[ch] + g)
            d_early = d_weight * weight
            w_ref[at, :] = d_early
            hi, lo = split2(d_early)
            hi_ref[at, :] = hi
            lo_ref[at, :] = lo
            return tuple(new)

        zero = jnp.zeros((8, SPAN), F32)
        acc = lax.fori_loop(0, CHUNKS, one, (zero, zero, zero))
        for ch in range(3):
            total = jnp.sum(acc[ch], axis=0, keepdims=True)
            if ch < 2:
                dp_ref[s, 6 + ch : 7 + ch, :] = total
            else:
                dpl_ref[s, 0:1, :] = total
        return 0

    lax.fori_loop(0, SEGS, backward_a, 0)

    later = onehot(iota((SPAN, SPAN), 0) > iota((SPAN, SPAN), 1))

    def back_sums(s, _):
        at = pl.ds(pl.multiple_of(s * PIX, PIX), PIX)
        x_ref[at, :] = mm(hi_ref[at, :], later) + mm(lo_ref[at, :], later)
        return 0

    lax.fori_loop(0, SEGS, back_sums, 0)

    def backward_b(s, _):
        def one(c, acc):
            at = place(s, c)
            q = pl.ds(pl.multiple_of(lax.rem(c, 4) * CHUNK, CHUNK), CHUNK)
            d = jnp.where(lane32 == 8 * s + 4 * (c // 4) + 3, q_ref[q, :], 0.0)
            d = jnp.sum(d, axis=1, keepdims=True)
            g0 = w_ref[at, :] - (x_ref[at, :] + d) * a_ref[at, :]
            dy = lines(s, c)
            g1 = g0 * dy
            g2 = g1 * dy
            return tuple(o + (g[0:16] + g[16:32]) for o, g in zip(acc, (g0, g1, g2)))

        zero = jnp.zeros((16, SPAN), F32)
        m0, m1, m2 = lax.fori_loop(0, CHUNKS, one, (zero, zero, zero))
        dx = delta_x(s)

        def down(x):
            return jnp.sum(x, axis=0, keepdims=True)

        s0, sx, sy = down(m0), down(m0 * dx), down(m1)
        sxx, sxy, syy = down(m0 * dx * dx), down(m1 * dx), down(m2)
        na, nb, nc = row(s, 2), row(s, 3), row(s, 4)
        dp_ref[s, 0:1, :] = -2.0 * na * sx - nb * sy
        dp_ref[s, 1:2, :] = -nb * sx - 2.0 * nc * sy
        dp_ref[s, 2:3, :] = 2.0 * na * sxx + nb * sxy
        dp_ref[s, 3:4, :] = 2.0 * nc * syy + nb * sxy
        dp_ref[s, 4:5, :] = -sxy * row(s, 9)
        dp_ref[s, 5:6, :] = s0 * row(s, 10)
        return 0

    lax.fori_loop(0, SEGS, backward_b, 0)

    main = jnp.concatenate([dp_ref[s] for s in range(SEGS)], axis=1)
    last = jnp.concatenate([dpl_ref[s, 0:1, :] for s in range(SEGS)], axis=1)
    send_buf[4] = pad_rows(spread(main, last, slot, e_ref[...])).T
    send(4)
    shown = q_ref[...].T
    for h in range(2):
        for ch in range(3):
            at = 32 + 4 * h + ch
            img_ref[ch, :, h * N : (h + 1) * N] = shown[at : at + 1]
    given = receive(4).T
    main = jnp.concatenate([given[8 * k : 8 * k + 8] for k in range(CAP)], axis=1)
    last = jnp.concatenate([given[64 + k : 65 + k] for k in range(CAP)], axis=1)
    grads = spread(main, last, high, ohj_ref[...])

    def adam(at, grad):
        moment = 0.9 * mom_ref[at] + 0.1 * grad
        second = 0.99 * sec_ref[at] + 0.01 * grad * grad
        nmom_ref[at] = moment
        nsec_ref[at] = second
        npar_ref[at] = par_ref[at] - 0.05 * moment / (jnp.sqrt(second) + 1e-08)

    for c in range(8):
        at = slice(c * N, (c + 1) * N)
        adam((slice(0, 8), at), grads[8 * c : 8 * c + 8])
        adam((slice(8, 9), at), grads[64 + c : 65 + c])

    for r in range(5):
        pltpu.make_async_remote_copy(
            src_ref=send_buf.at[r, pl.ds(0, N - 1)],
            dst_ref=recv_buf.at[r, pl.ds(0, N - 1)],
            send_sem=send_sem.at[r],
            recv_sem=recv_sem.at[r],
            device_id=(lax.rem(me + 1, N),),
            device_id_type=MESH,
        ).wait_send()


def nat_pad(x):
    return jnp.concatenate([x, jnp.zeros((16 - x.shape[0], x.shape[1]), BF16)], axis=0)


def per_device(params, moment, second, fetch_ids, seg_ids, seg_count, seg_perm, target):
    vmem = pl.BlockSpec(memory_space=pltpu.VMEM)
    smem = pl.BlockSpec(memory_space=pltpu.SMEM)
    shape = jax.ShapeDtypeStruct
    image, new_params, new_moment, new_second = pl.pallas_call(
        kernel,
        out_shape=(
            shape((3, 1, PIX), F32),
            shape(params.shape, F32),
            shape(params.shape, F32),
            shape(params.shape, F32),
        ),
        in_specs=[smem, smem] + [vmem] * 7,
        out_specs=(vmem,) * 4,
        scratch_shapes=[
            pltpu.VMEM((5, N, N), F32),
            pltpu.VMEM((5, N, N), F32),
            pltpu.VMEM((SEGS * SPAN, N), BF16),
            pltpu.VMEM((N, SEGS * SPAN), BF16),
            pltpu.VMEM((4 * N, SEGS * N), BF16),
            pltpu.VMEM((SEGS * N, 4 * N), BF16),
            pltpu.VMEM((CAP * N, N), BF16),
            pltpu.VMEM((SEGS, 16, SPAN), F32),
            pltpu.VMEM((N, N), F32),
            pltpu.VMEM((N, N), F32),
            pltpu.VMEM((SEGS * PIX, SPAN), F32),
            pltpu.VMEM((SEGS * PIX, SPAN), F32),
            pltpu.VMEM((SEGS * PIX, SPAN), BF16),
            pltpu.VMEM((SEGS * PIX, SPAN), BF16),
            pltpu.VMEM((SEGS * PIX, SPAN), F32),
            pltpu.VMEM((SEGS, 8, SPAN), F32),
            pltpu.VMEM((SEGS, 8, SPAN), F32),
            pltpu.SemaphoreType.DMA((5,)),
            pltpu.SemaphoreType.DMA((5,)),
        ],
        compiler_params=pltpu.CompilerParams(collective_id=0, has_side_effects=True),
        name="splat_step",
    )(
        seg_count,
        seg_perm,
        params,
        moment,
        second,
        fetch_ids[0].T,
        seg_ids,
        seg_perm.reshape(SEGS, N),
        jnp.transpose(target, (1, 0, 2)),
    )
    return (jnp.transpose(image, (1, 0, 2)), new_params, new_moment, new_second)


def solution(mesh):
    placed = (
        P(None, "dev"),
        P(None, "dev"),
        P(None, "dev"),
        P("dev", None, None),
        P("dev", None),
        P("dev"),
        P(),
        P("dev", None, None),
    )
    return jax.shard_map(
        per_device,
        mesh=mesh,
        in_specs=placed,
        out_specs=(P("dev", None, None), P(None, "dev"), P(None, "dev"), P(None, "dev")),
        check_vma=False,
    )
```

time: 894 us -> 66.1 us (0.07)
  waiting for transfers between devices: 665 us -> 0 us
  blocking collectives: 69.4 us -> 0 us
  Pallas kernels: 0 us -> 60.9 us
  other arithmetic: 59.6 us -> 0 us
  local copies, waits for them, and re-layouts: 49.9 us -> 4.23 us
  starting transfers between devices: 16.3 us -> 0 us
  between operations: 14.5 us -> 0.65 us
  matrix products: 11.6 us -> 0 us
    reduce_scatter x1 -> x0, waiting for transfers between devices: 646 us -> none  [per_device(): grad = lax.psum_scatter(dense, 'dev', scatter_dimension=1, tiled=True)]
    all_gather x2 -> x0, blocking collectives: 69.4 us -> none  [the longest x1 35.8 us: per_device(): lax.all_gather(logs, 'dev', axis=0, tiled=True)]
    pallas_call x0 -> x1, Pallas kernels: none -> 60.9 us  [per_device(): pl.pallas_call(kernel, out_shape=(shape((3, 1, PIX), F32), shape(params.s...]
    scatter-add x4 -> x0, other arithmetic: 52.4 us -> none  [the longest x3 46.1 us: per_device(): jnp.zeros((nparam, ndev * owned), jnp.float32).at[:, global_ids]]
    scatter-add x2 -> x0, local copies, waits for them, and re-layouts: 36.9 us -> none  [per_device(): jnp.zeros((nparam, ndev * owned), jnp.float32).at[:, global_ids]]
    all_to_all x2 -> x0, waiting for transfers between devices: 18.7 us -> none  [the longest x1 13.5 us: per_device(): lax.all_to_all(buckets, 'dev', split_axis=1, concat_axis=1, tiled=True)]
    all_to_all x2 -> x0, starting transfers between devices: 16.2 us -> none  [the longest x1 11.5 us: per_device(): lax.all_to_all(wanted, 'dev', split_axis=0, concat_axis=0, tiled=True)]
    dot_general x9 -> x0, matrix products: 11.6 us -> none  [the longest x2 4.46 us: segment(): earlier = jnp.dot(lower, logt, precision=lax.Precision.HIGHEST)]
  transfers between devices with their start and end apart: 4 -> 0, of which waited for: 3 -> 0; matrix products, arithmetic and copies ran while one was open for 1% -> 0% of each run, Pallas kernels for 0% -> 0%
where the time goes in v2:
time: 66.1 us; the launch traced here: 65.8 us
  Pallas kernels  60.9 us (92%)
  local copies, waits for them, and re-layouts  4.23 us (6%)
    pallas_call x1, Pallas kernels, per_device(): pl.pallas_call(kernel, out_shape=(shape((3, 1, PIX), F32), shape(params.s...  60.9 us
    unnamed x10, local copies, waits for them, and re-layouts  4.23 us

profile of v2, /device:TPU:1, one launch (start us, length us, event | category | flops | bytes accessed | tf_op | source)
XLA Modules:
  0.0 65.8 jit_solution(12299433756340305029)
XLA Ops:
  0.6 60.9 %splat_step.1 = (f32[3,1,256]{2,1,0:T(1,128)}, f32[9,1024]{1,0:T(8,128)}, f32[9,1024]{1,0:T(8,128)}, f32[9,1024]{1,0:T(8,128)}) custom-call(s32[4]{0:T(128)} %count_ref.1, s32[512]{0:T(512)} %perm_ref.1, f32[9,1024]{1,0:T(8,128)} %par_ref.1, f32[9,1024]{1,0:T(8,128)} %mom_ref.1, f32[9,1024]{1,0:T(8,128)} %sec_ref.1, s32[8,128]{1,0:T(8,128)} %bitcast.7, ...), custom_call_target="tpu_custom_call" | custom-call | tf_op jit(solution)/shard_map/splat_step/pallas_call | solution.py:430
  61.6 0.0 copy-start.2
  61.6 0.7 copy-done.2
  62.2 0.6 copy.16
  62.8 0.0 copy-start.1
  62.8 1.5 %copy.17 = f32[9,1024]{1,0:T(8,128)} copy(f32[9,1024]{1,0:T(8,128)} %get-tuple-element.17) | data formatting | bytes 73728
  64.3 0.0 copy-done.1
  64.3 0.0 copy-start
  64.3 0.6 copy.18
  64.9 0.2 copy-done
  65.2 0.6 copy.19
Async XLA Ops:
  61.6 0.7 %copy-start.2 = (f32[3,1,256]{2,1,0:T(1,128)S(1)}, f32[3,1,256]{2,1,0:T(1,128)}, u32[]{:S(2)}) copy-start(f32[3,1,256]{2,1,0:T(1,128)} %get-tuple-element.8) | copy-start | bytes 9220
  62.8 1.5 %copy-start.1 = (f32[9,1024]{1,0:T(8,128)S(1)}, f32[9,1024]{1,0:T(8,128)}, u32[]{:S(2)}) copy-start(f32[9,1024]{1,0:T(8,128)} %get-tuple-element.18) | copy-start | bytes 110596
  64.3 0.9 %copy-start = (f32[9,1024]{1,0:T(8,128)S(1)}, f32[9,1024]{1,0:T(8,128)}, u32[]{:S(2)}) copy-start(f32[9,1024]{1,0:T(8,128)} %get-tuple-element.19) | copy-start | bytes 110596

commit v3 on v2

--- a/solution.py
+++ b/solution.py
@@ -75,11 +75,7 @@
 
 
 def kernel(
-    count_ref, perm_ref, par_ref, mom_ref, sec_ref, fetch_ref, ids_ref, permv_ref, tgt_ref,
-    img_ref, npar_ref, nmom_ref, nsec_ref,
-    send_buf, recv_buf, e_ref, et_ref, o_ref, ot_ref, ohj_ref, rows_ref, f_ref, q_ref,
-    a_ref, w_ref, hi_ref, lo_ref, x_ref, dp_ref, dpl_ref,
-    send_sem, recv_sem,
+    count_hbm, perm_hbm, par_hbm, fetch_hbm, ids_hbm, permv_hbm, tgt_hbm, img_ref, grad_ref, send_buf, recv_buf, e_ref, et_ref, o_ref, ot_ref, ohj_ref, rows_ref, f_ref, q_ref, a_ref, w_ref, hi_ref, lo_ref, x_ref, dp_ref, dpl_ref, count_ref, perm_ref, par_ref, fetch_ref, ids_ref, permv_ref, tgt_ref, send_sem, recv_sem, in_sem,
 ):
     me = lax.axis_index("dev")
     barrier = pltpu.get_barrier_semaphore()
@@ -91,21 +87,46 @@
         return 0
 
     lax.fori_loop(1, N, greet, 0)
+    pairs = (
+        (fetch_hbm, fetch_ref), (ids_hbm, ids_ref), (par_hbm, par_ref), (permv_hbm, permv_ref),
+        (perm_hbm, perm_ref), (count_hbm, count_ref), (tgt_hbm, tgt_ref),
+    )
+    for n, (src, dst) in enumerate(pairs):
+        pltpu.make_async_copy(src, dst, in_sem.at[n]).start()
+    for n, (src, dst) in enumerate(pairs):
+        pltpu.make_async_copy(src, dst, in_sem.at[n]).wait()
+
+    X, Y = me // 32, lax.rem(me // 8, 4)
+    Z, C = lax.rem(me // 2, 4), lax.rem(me, 2)
+    near = [
+        lax.rem(Z + dz, 4) * 2 + lax.rem(C + dc, 2)
+        for dz in (2, 1, 3, 0)
+        for dc in (0, 1)
+    ]
+
+    def push(r, to):
+        pltpu.make_async_remote_copy(
+            src_ref=send_buf.at[r, pl.ds(to, 1)],
+            dst_ref=recv_buf.at[r, pl.ds(me, 1)],
+            send_sem=send_sem.at[r],
+            recv_sem=recv_sem.at[r],
+            device_id=(to,),
+            device_id_type=MESH,
+        ).start()
+
+    def ring(j):
+        return lax.rem(2 + j * (j + 1) // 2, 4)
 
     def send(r):
-        def one(i, _):
-            to = lax.rem(me + i, N)
-            pltpu.make_async_remote_copy(
-                src_ref=send_buf.at[r, pl.ds(to, 1)],
-                dst_ref=recv_buf.at[r, pl.ds(me, 1)],
-                send_sem=send_sem.at[r],
-                recv_sem=recv_sem.at[r],
-                device_id=(to,),
-                device_id_type=MESH,
-            ).start()
+        def column(i, _):
+            base = lax.rem(X + ring(i // 4), 4) * 32 + lax.rem(Y + ring(lax.rem(i, 4)), 4) * 8
+            for at in near:
+                push(r, base + at)
             return 0
 
-        lax.fori_loop(1, N, one, 0)
+        lax.fori_loop(0, 15, column, 0, unroll=True)
+        for at in near[:6] + near[7:]:
+            push(r, X * 32 + Y * 8 + at)
         pltpu.make_async_copy(
             send_buf.at[r, pl.ds(me, 1)], recv_buf.at[r, pl.ds(me, 1)], recv_sem.at[r]
         ).start()
@@ -113,10 +134,6 @@
     def receive(r):
         pltpu.make_async_copy(send_buf.at[r], recv_buf.at[r], recv_sem.at[r]).wait()
         return recv_buf[r]
-
-    send_buf[0] = pad_rows(fetch_ref[...].astype(F32)).T
-    pl.semaphore_wait(barrier, N - 1)
-    send(0)
 
     ids = [ids_ref[s : s + 1, :] for s in range(SEGS)]
     for s in range(SEGS):
@@ -131,21 +148,10 @@
     table += [par_ref[8:9, c * N : (c + 1) * N] for c in range(8)]
     table = jnp.concatenate(table, axis=0)
 
-    got = receive(0).astype(I32)
-    wanted = got.astype(F32).T[0:8].astype(I32)
-    wanted = jnp.concatenate([wanted[k : k + 1] for k in range(CAP)], axis=1)
-    high = wanted // N
-    low = wanted % N
-    oht = onehot(iota((N, CAP * N), 0) == low)
-    main, last = pick(table, oht, high)
-    out = [main[:, k * N : (k + 1) * N] for k in range(CAP)]
-    out += [last[:, k * N : (k + 1) * N] for k in range(CAP)]
-    send_buf[1] = pad_rows(jnp.concatenate(out, axis=0)).T
-    send(1)
-
-    lane = iota((N, N), 1)
-    for k in range(CAP):
-        ohj_ref[k * N : (k + 1) * N, :] = onehot(got[:, k : k + 1] % N == lane)
+    send_buf[0] = pad_rows(fetch_ref[...].astype(F32)).T
+    pl.semaphore_wait(barrier, N - 1)
+    send(0)
+
     nat = permv_ref[...]
     nat = jnp.concatenate([nat // SEGS, nat % SEGS], axis=0).astype(F32).astype(BF16)
     col = iota((N, SEGS * N), 1)
@@ -169,6 +175,21 @@
     tgt = jnp.concatenate([jnp.zeros((32, N), F32)] + tgt, axis=0)
     f_ref[...] = pad_rows(tgt).T
 
+    got = receive(0).astype(I32)
+    wanted = got.astype(F32).T[0:8].astype(I32)
+    wanted = jnp.concatenate([wanted[k : k + 1] for k in range(CAP)], axis=1)
+    high = wanted // N
+    low = wanted % N
+    oht = onehot(iota((N, CAP * N), 0) == low)
+    main, last = pick(table, oht, high)
+    out = [main[:, k * N : (k + 1) * N] for k in range(CAP)]
+    out += [last[:, k * N : (k + 1) * N] for k in range(CAP)]
+    send_buf[1] = pad_rows(jnp.concatenate(out, axis=0)).T
+    send(1)
+
+    lane = iota((N, N), 1)
+    for k in range(CAP):
+        ohj_ref[k * N : (k + 1) * N, :] = onehot(got[:, k : k + 1] % N == lane)
     arrived = receive(1).T
     main, last = pick(arrived[0:72], et_ref[...], slot)
     scale = jnp.exp(main)
@@ -239,9 +260,9 @@
             )
             return 0
 
-        return lax.fori_loop(0, CHUNKS, one, 0)
-
-    lax.fori_loop(0, SEGS, forward_a, 0)
+        return lax.fori_loop(0, CHUNKS, one, 0, unroll=True)
+
+    lax.fori_loop(0, SEGS, forward_a, 0, unroll=True)
 
     tri = iota((SPAN, SPAN), 0) < iota((SPAN, SPAN), 1)
     earlier = onehot(tri)
@@ -251,7 +272,7 @@
         x_ref[at, :] = mm(hi_ref[at, :], earlier) + mm(lo_ref[at, :], earlier)
         return 0
 
-    lax.fori_loop(0, SEGS, sums, 0)
+    lax.fori_loop(0, SEGS, sums, 0, unroll=True)
 
     def forward_b(s, _):
         def one(c, _):
@@ -268,9 +289,9 @@
             f_ref[q, :] = kept
             return 0
 
-        return lax.fori_loop(0, CHUNKS, one, 0)
-
-    lax.fori_loop(0, SEGS, forward_b, 0)
+        return lax.fori_loop(0, CHUNKS, one, 0, unroll=True)
+
+    lax.fori_loop(0, SEGS, forward_b, 0, unroll=True)
 
     send_buf[2] = f_ref[...]
     send(2)
@@ -330,7 +351,7 @@
             return tuple(new)
 
         zero = jnp.zeros((8, SPAN), F32)
-        acc = lax.fori_loop(0, CHUNKS, one, (zero, zero, zero))
+        acc = lax.fori_loop(0, CHUNKS, one, (zero, zero, zero), unroll=True)
         for ch in range(3):
             total = jnp.sum(acc[ch], axis=0, keepdims=True)
             if ch < 2:
@@ -339,7 +360,7 @@
                 dpl_ref[s, 0:1, :] = total
         return 0
 
-    lax.fori_loop(0, SEGS, backward_a, 0)
+    lax.fori_loop(0, SEGS, backward_a, 0, unroll=True)
 
     later = onehot(iota((SPAN, SPAN), 0) > iota((SPAN, SPAN), 1))
 
@@ -348,7 +369,7 @@
         x_ref[at, :] = mm(hi_ref[at, :], later) + mm(lo_ref[at, :], later)
         return 0
 
-    lax.fori_loop(0, SEGS, back_sums, 0)
+    lax.fori_loop(0, SEGS, back_sums, 0, unroll=True)
 
     def backward_b(s, _):
         def one(c, acc):
@@ -363,7 +384,7 @@
             return tuple(o + (g[0:16] + g[16:32]) for o, g in zip(acc, (g0, g1, g2)))
 
         zero = jnp.zeros((16, SPAN), F32)
-        m0, m1, m2 = lax.fori_loop(0, CHUNKS, one, (zero, zero, zero))
+        m0, m1, m2 = lax.fori_loop(0, CHUNKS, one, (zero, zero, zero), unroll=True)
         dx = delta_x(s)
 
         def down(x):
@@ -380,7 +401,7 @@
         dp_ref[s, 5:6, :] = s0 * row(s, 10)
         return 0
 
-    lax.fori_loop(0, SEGS, backward_b, 0)
+    lax.fori_loop(0, SEGS, backward_b, 0, unroll=True)
 
     main = jnp.concatenate([dp_ref[s] for s in range(SEGS)], axis=1)
     last = jnp.concatenate([dpl_ref[s, 0:1, :] for s in range(SEGS)], axis=1)
@@ -396,17 +417,7 @@
     last = jnp.concatenate([given[64 + k : 65 + k] for k in range(CAP)], axis=1)
     grads = spread(main, last, high, ohj_ref[...])
 
-    def adam(at, grad):
-        moment = 0.9 * mom_ref[at] + 0.1 * grad
-        second = 0.99 * sec_ref[at] + 0.01 * grad * grad
-        nmom_ref[at] = moment
-        nsec_ref[at] = second
-        npar_ref[at] = par_ref[at] - 0.05 * moment / (jnp.sqrt(second) + 1e-08)
-
-    for c in range(8):
-        at = slice(c * N, (c + 1) * N)
-        adam((slice(0, 8), at), grads[8 * c : 8 * c + 8])
-        adam((slice(8, 9), at), grads[64 + c : 65 + c])
+    grad_ref[...] = grads
 
     for r in range(5):
         pltpu.make_async_remote_copy(
@@ -419,24 +430,37 @@
         ).wait_send()
 
 
+def update(
+    grad_ref, img_ref, par_ref, mom_ref, sec_ref, oimg_ref, npar_ref, nmom_ref, nsec_ref
+):
+    oimg_ref[...] = img_ref[...]
+
+    def adam(at, grad):
+        moment = 0.9 * mom_ref[at] + 0.1 * grad
+        second = 0.99 * sec_ref[at] + 0.01 * grad * grad
+        nmom_ref[at] = moment
+        nsec_ref[at] = second
+        npar_ref[at] = par_ref[at] - 0.05 * moment / (jnp.sqrt(second) + 1e-08)
+
+    for c in range(8):
+        at = slice(c * N, (c + 1) * N)
+        adam((slice(0, 8), at), grad_ref[8 * c : 8 * c + 8])
+        adam((slice(8, 9), at), grad_ref[64 + c : 65 + c])
+
+
 def nat_pad(x):
     return jnp.concatenate([x, jnp.zeros((16 - x.shape[0], x.shape[1]), BF16)], axis=0)
 
 
 def per_device(params, moment, second, fetch_ids, seg_ids, seg_count, seg_perm, target):
     vmem = pl.BlockSpec(memory_space=pltpu.VMEM)
-    smem = pl.BlockSpec(memory_space=pltpu.SMEM)
+    hbm = pl.BlockSpec(memory_space=pltpu.HBM)
     shape = jax.ShapeDtypeStruct
-    image, new_params, new_moment, new_second = pl.pallas_call(
+    image, grads = pl.pallas_call(
         kernel,
-        out_shape=(
-            shape((3, 1, PIX), F32),
-            shape(params.shape, F32),
-            shape(params.shape, F32),
-            shape(params.shape, F32),
-        ),
-        in_specs=[smem, smem] + [vmem] * 7,
-        out_specs=(vmem,) * 4,
+        out_shape=(shape((3, 1, PIX), F32), shape((72, N), F32)),
+        in_specs=[hbm] * 7,
+        out_specs=(vmem,) * 2,
         scratch_shapes=[
             pltpu.VMEM((5, N, N), F32),
             pltpu.VMEM((5, N, N), F32),
@@ -455,8 +479,16 @@
             pltpu.VMEM((SEGS * PIX, SPAN), F32),
             pltpu.VMEM((SEGS, 8, SPAN), F32),
             pltpu.VMEM((SEGS, 8, SPAN), F32),
+            pltpu.SMEM((SEGS,), I32),
+            pltpu.SMEM((SEGS * N,), I32),
+            pltpu.VMEM(params.shape, F32),
+            pltpu.VMEM((CAP, N), I32),
+            pltpu.VMEM((SEGS, SPAN), I32),
+            pltpu.VMEM((SEGS, N), I32),
+            pltpu.VMEM((3, 1, PIX), F32),
             pltpu.SemaphoreType.DMA((5,)),
             pltpu.SemaphoreType.DMA((5,)),
+            pltpu.SemaphoreType.DMA((7,)),
         ],
         compiler_params=pltpu.CompilerParams(collective_id=0, has_side_effects=True),
         name="splat_step",
@@ -464,13 +496,18 @@
         seg_count,
         seg_perm,
         params,
-        moment,
-        second,
         fetch_ids[0].T,
         seg_ids,
         seg_perm.reshape(SEGS, N),
         jnp.transpose(target, (1, 0, 2)),
     )
+    image, new_params, new_moment, new_second = pl.pallas_call(
+        update,
+        out_shape=(shape((3, 1, PIX), F32),) + (shape(params.shape, F32),) * 3,
+        in_specs=[vmem] * 5,
+        out_specs=(vmem,) * 4,
+        name="adam",
+    )(grads, image, params, moment, second)
     return (jnp.transpose(image, (1, 0, 2)), new_params, new_moment, new_second)
 
 

time: 66.1 us -> 47.2 us (0.71)
  Pallas kernels: 60.9 us -> 46.4 us
  local copies, waits for them, and re-layouts: 4.23 us -> 0 us
    pallas_call x1 -> x2, Pallas kernels: 60.9 us -> 46.4 us  [the longest x1 44.7 us: per_device(): pl.pallas_call(kernel, out_shape=(shape((3, 1, PIX), F32), shape((72, N),...]
    unnamed x10 -> x0, local copies, waits for them, and re-layouts: 4.23 us -> none
where the time goes in v3:
time: 47.2 us; the launch traced here: 47 us
  Pallas kernels  46.4 us (98%)
  between operations  0.64 us (1%)
    pallas_call x1, Pallas kernels, per_device(): pl.pallas_call(kernel, out_shape=(shape((3, 1, PIX), F32), shape((72, N),...  44.7 us
    pallas_call x1, Pallas kernels, per_device(): pl.pallas_call(update, out_shape=(shape((3, 1, PIX), F32),) + (shape(para...  1.64 us

profile of v3, /device:TPU:1, one launch (start us, length us, event | category | flops | bytes accessed | tf_op | source)
XLA Modules:
  0.0 47.0 jit_solution(2687477834136197541)
XLA Ops:
  0.6 44.7 %splat_step.1 = (f32[3,1,256]{2,1,0:T(1,128)}, f32[72,128]{1,0:T(8,128)}) custom-call(s32[4]{0:T(128)} %count_hbm.1, s32[512]{0:T(512)} %perm_hbm.1, f32[9,1024]{1,0:T(8,128)} %par_ref.1, s32[8,128]{1,0:T(8,128)} %bitcast.7, s32[4,256]{1,0:T(4,128)} %ids_hbm.1, s32[4,128]{1,0:T(4,128)} %bitcast.6, f32[3,1,256]{2,1,0:T(1,128)} %bitcast.8), custom_call_target="tpu_custom_call" | custom-call | tf_op jit(solution)/shard_map/splat_step/pallas_call | solution.py:459
  45.4 1.6 %adam.1 = (f32[3,1,256]{2,1,0:T(1,128)}, f32[9,1024]{1,0:T(8,128)}, f32[9,1024]{1,0:T(8,128)}, f32[9,1024]{1,0:T(8,128)}) custom-call(f32[72,128]{1,0:T(8,128)} %get-tuple-element.10.grad_ref, f32[3,1,256]{2,1,0:T(1,128)} %get-tuple-element.11.img_ref, f32[9,1024]{1,0:T(8,128)} %par_ref.1, f32[9,1024]{1,0:T(8,128)} %mom_ref.1, f32[9,1024]{1,0:T(8,128)} %sec_ref.1), custom_call_target="tpu_custom_call" | custom-call | tf_op jit(solution)/shard_map/adam/pallas_call | solution.py:504

commit v4 on v3

--- a/solution.py
+++ b/solution.py
@@ -14,6 +14,13 @@
 CHUNK = 32
 CHUNKS = PIX // CHUNK
 CAP = 8
+FAR_FIRST = sorted(
+    (-min(a, 4 - a) - min(b, 4 - b) - min(c // 2, 4 - c // 2), a, b, c)
+    for a in range(4)
+    for b in range(4)
+    for c in range(8)
+    if a or b or c
+)
 
 
 def iota(shape, axis):
@@ -75,34 +82,27 @@
 
 
 def kernel(
-    count_hbm, perm_hbm, par_hbm, fetch_hbm, ids_hbm, permv_hbm, tgt_hbm, img_ref, grad_ref, send_buf, recv_buf, e_ref, et_ref, o_ref, ot_ref, ohj_ref, rows_ref, f_ref, q_ref, a_ref, w_ref, hi_ref, lo_ref, x_ref, dp_ref, dpl_ref, count_ref, perm_ref, par_ref, fetch_ref, ids_ref, permv_ref, tgt_ref, send_sem, recv_sem, in_sem,
+    count_hbm, perm_hbm, par_hbm, fetch_hbm, ids_hbm, permv_hbm, tgt_hbm, mom_hbm, sec_hbm, img_ref, npar_ref, nmom_ref, nsec_ref, send_buf, recv_buf, e_ref, et_ref, o_ref, ot_ref, ohj_ref, rows_ref, f_ref, q_ref, a_ref, w_ref, hi_ref, lo_ref, x_ref, dp_ref, dpl_ref, count_ref, perm_ref, par_ref, fetch_ref, ids_ref, permv_ref, tgt_ref, mom_ref, sec_ref, send_sem, recv_sem, in_sem,
 ):
     me = lax.axis_index("dev")
     barrier = pltpu.get_barrier_semaphore()
 
-    def greet(i, _):
-        pl.semaphore_signal(
-            barrier, inc=1, device_id=(lax.rem(me + i, N),), device_id_type=MESH
-        )
-        return 0
-
-    lax.fori_loop(1, N, greet, 0)
+    X, Y = me // 32, lax.rem(me // 8, 4)
+    Z, C = lax.rem(me // 2, 4), lax.rem(me, 2)
+    planes = [[lax.rem(X + d, 4) * 32 for d in range(4)], [lax.rem(Y + d, 4) * 8 for d in range(4)]]
+    near = [lax.rem(Z + d // 2, 4) * 2 + lax.rem(C + d, 2) for d in range(8)]
+    others = [planes[0][a] + planes[1][b] + near[c] for _, a, b, c in FAR_FIRST]
+    for to in others:
+        pl.semaphore_signal(barrier, inc=1, device_id=(to,), device_id_type=MESH)
     pairs = (
         (fetch_hbm, fetch_ref), (ids_hbm, ids_ref), (par_hbm, par_ref), (permv_hbm, permv_ref),
-        (perm_hbm, perm_ref), (count_hbm, count_ref), (tgt_hbm, tgt_ref),
+        (perm_hbm, perm_ref), (count_hbm, count_ref), (tgt_hbm, tgt_ref), (mom_hbm, mom_ref),
+        (sec_hbm, sec_ref),
     )
     for n, (src, dst) in enumerate(pairs):
         pltpu.make_async_copy(src, dst, in_sem.at[n]).start()
     for n, (src, dst) in enumerate(pairs):
         pltpu.make_async_copy(src, dst, in_sem.at[n]).wait()
-
-    X, Y = me // 32, lax.rem(me // 8, 4)
-    Z, C = lax.rem(me // 2, 4), lax.rem(me, 2)
-    near = [
-        lax.rem(Z + dz, 4) * 2 + lax.rem(C + dc, 2)
-        for dz in (2, 1, 3, 0)
-        for dc in (0, 1)
-    ]
 
     def push(r, to):
         pltpu.make_async_remote_copy(
@@ -114,19 +114,9 @@
             device_id_type=MESH,
         ).start()
 
-    def ring(j):
-        return lax.rem(2 + j * (j + 1) // 2, 4)
-
     def send(r):
-        def column(i, _):
-            base = lax.rem(X + ring(i // 4), 4) * 32 + lax.rem(Y + ring(lax.rem(i, 4)), 4) * 8
-            for at in near:
-                push(r, base + at)
-            return 0
-
-        lax.fori_loop(0, 15, column, 0, unroll=True)
-        for at in near[:6] + near[7:]:
-            push(r, X * 32 + Y * 8 + at)
+        for to in others:
+            push(r, to)
         pltpu.make_async_copy(
             send_buf.at[r, pl.ds(me, 1)], recv_buf.at[r, pl.ds(me, 1)], recv_sem.at[r]
         ).start()
@@ -417,7 +407,18 @@
     last = jnp.concatenate([given[64 + k : 65 + k] for k in range(CAP)], axis=1)
     grads = spread(main, last, high, ohj_ref[...])
 
-    grad_ref[...] = grads
+
+    def adam(at, grad):
+        moment = 0.9 * mom_ref[at] + 0.1 * grad
+        second = 0.99 * sec_ref[at] + 0.01 * grad * grad
+        nmom_ref[at] = moment
+        nsec_ref[at] = second
+        npar_ref[at] = par_ref[at] - 0.05 * moment / (jnp.sqrt(second) + 1e-08)
+
+    for c in range(8):
+        at = slice(c * N, (c + 1) * N)
+        adam((slice(0, 8), at), grads[8 * c : 8 * c + 8])
+        adam((slice(8, 9), at), grads[64 + c : 65 + c])
 
     for r in range(5):
         pltpu.make_async_remote_copy(
@@ -430,22 +431,13 @@
         ).wait_send()
 
 
-def update(
-    grad_ref, img_ref, par_ref, mom_ref, sec_ref, oimg_ref, npar_ref, nmom_ref, nsec_ref
-):
-    oimg_ref[...] = img_ref[...]
-
-    def adam(at, grad):
-        moment = 0.9 * mom_ref[at] + 0.1 * grad
-        second = 0.99 * sec_ref[at] + 0.01 * grad * grad
-        nmom_ref[at] = moment
-        nsec_ref[at] = second
-        npar_ref[at] = par_ref[at] - 0.05 * moment / (jnp.sqrt(second) + 1e-08)
-
-    for c in range(8):
-        at = slice(c * N, (c + 1) * N)
-        adam((slice(0, 8), at), grad_ref[8 * c : 8 * c + 8])
-        adam((slice(8, 9), at), grad_ref[64 + c : 65 + c])
+def store(*refs):
+    sems = refs[8]
+    copies = [pltpu.make_async_copy(refs[i], refs[4 + i], sems.at[i]) for i in range(4)]
+    for copy in copies:
+        copy.start()
+    for copy in copies:
+        copy.wait()
 
 
 def nat_pad(x):
@@ -456,11 +448,11 @@
     vmem = pl.BlockSpec(memory_space=pltpu.VMEM)
     hbm = pl.BlockSpec(memory_space=pltpu.HBM)
     shape = jax.ShapeDtypeStruct
-    image, grads = pl.pallas_call(
+    results = pl.pallas_call(
         kernel,
-        out_shape=(shape((3, 1, PIX), F32), shape((72, N), F32)),
-        in_specs=[hbm] * 7,
-        out_specs=(vmem,) * 2,
+        out_shape=(shape((3, 1, PIX), F32),) + (shape(params.shape, F32),) * 3,
+        in_specs=[hbm] * 9,
+        out_specs=(vmem,) * 4,
         scratch_shapes=[
             pltpu.VMEM((5, N, N), F32),
             pltpu.VMEM((5, N, N), F32),
@@ -486,28 +478,41 @@
             pltpu.VMEM((SEGS, SPAN), I32),
             pltpu.VMEM((SEGS, N), I32),
             pltpu.VMEM((3, 1, PIX), F32),
+            pltpu.VMEM(params.shape, F32),
+            pltpu.VMEM(params.shape, F32),
             pltpu.SemaphoreType.DMA((5,)),
             pltpu.SemaphoreType.DMA((5,)),
-            pltpu.SemaphoreType.DMA((7,)),
+            pltpu.SemaphoreType.DMA((9,)),
         ],
-        compiler_params=pltpu.CompilerParams(collective_id=0, has_side_effects=True),
+        compiler_params=pltpu.CompilerParams(
+            collective_id=0, has_side_effects=True, vmem_limit_bytes=32 << 20
+        ),
         name="splat_step",
     )(
-        seg_count,
-        seg_perm,
-        params,
-        fetch_ids[0].T,
-        seg_ids,
-        seg_perm.reshape(SEGS, N),
-        jnp.transpose(target, (1, 0, 2)),
+        *(
+            pltpu.with_memory_space_constraint(x, pltpu.HBM)
+            for x in (
+                seg_count,
+                seg_perm,
+                params,
+                fetch_ids[0].T,
+                seg_ids,
+                seg_perm.reshape(SEGS, N),
+                jnp.transpose(target, (1, 0, 2)),
+                moment,
+                second,
+            )
+        )
     )
     image, new_params, new_moment, new_second = pl.pallas_call(
-        update,
-        out_shape=(shape((3, 1, PIX), F32),) + (shape(params.shape, F32),) * 3,
-        in_specs=[vmem] * 5,
-        out_specs=(vmem,) * 4,
-        name="adam",
-    )(grads, image, params, moment, second)
+        store,
+        out_shape=[shape(x.shape, F32) for x in results],
+        in_specs=[vmem] * 4,
+        out_specs=[hbm] * 4,
+        scratch_shapes=[pltpu.SemaphoreType.DMA((4,))],
+        compiler_params=pltpu.CompilerParams(vmem_limit_bytes=1 << 20),
+        name="store",
+    )(*results)
     return (jnp.transpose(image, (1, 0, 2)), new_params, new_moment, new_second)
 
 

time: 47.2 us -> 44.5 us (0.943)
  Pallas kernels: 46.4 us -> 43.6 us
    pallas_call x2, Pallas kernels: 46.4 us -> 43.6 us  [the longest x1 42.9 us: per_device(): pl.pallas_call(kernel, out_shape=(shape((3, 1, PIX), F32),) + (shape(para...]
where the time goes in v4:
time: 44.5 us; the launch traced here: 44.3 us
  Pallas kernels  43.6 us (98%)
  between operations  0.64 us (1%)
    pallas_call x1, Pallas kernels, per_device(): pl.pallas_call(kernel, out_shape=(shape((3, 1, PIX), F32),) + (shape(para...  42.9 us

profile of v4, /device:TPU:1, one launch (start us, length us, event | category | flops | bytes accessed | tf_op | source)
XLA Modules:
  0.0 44.3 jit_solution(7828384773258944892)
XLA Ops:
  0.6 42.9 %splat_step.1 = (f32[3,1,256]{2,1,0:T(1,128)S(1)}, f32[9,1024]{1,0:T(8,128)S(1)}, f32[9,1024]{1,0:T(8,128)S(1)}, f32[9,1024]{1,0:T(8,128)S(1)}) custom-call(s32[4]{0:T(128)} %count_hbm.1, s32[512]{0:T(512)} %perm_hbm.1, f32[9,1024]{1,0:T(8,128)} %par_hbm.1, s32[8,128]{1,0:T(8,128)} %bitcast.7, s32[4,256]{1,0:T(4,128)} %ids_hbm.1, s32[4,128]{1,0:T(4,128)} %bitcast.6, ...), custom_call_target="tpu_custom_call" | custom-call | tf_op jit(solution)/shard_map/splat_step/pallas_call | solution.py:451
  43.6 0.7 %store.1 = (f32[3,1,256]{2,1,0:T(1,128)}, f32[9,1024]{1,0:T(8,128)}, f32[9,1024]{1,0:T(8,128)}, f32[9,1024]{1,0:T(8,128)}) custom-call(f32[3,1,256]{2,1,0:T(1,128)S(1)} %get-tuple-element.12.refs_0_, f32[9,1024]{1,0:T(8,128)S(1)} %get-tuple-element.13.refs_1_, f32[9,1024]{1,0:T(8,128)S(1)} %get-tuple-element.14.refs_2_, f32[9,1024]{1,0:T(8,128)S(1)} %get-tuple-element.15.refs_3_), custom_call_target="tpu_custom_call" | custom-call | tf_op jit(solution)/shard_map/store/pallas_call | solution.py:507
